TPU v7x, 32 devices: a whole 2x2x4 slice. The times are simulated.
32 devices in a mesh: groups: 2 (over x), tile: 16 (over z, y, core).
Axes of the slice: x: 2, y: 2, z: 4, core: 2. Of those that a mesh axis runs over, the one named last changes fastest.
Arguments:
- fine_nodes: bfloat16 [32768, 512], P(('groups', 'tile')), parts along dimension 0, may hold values from -6 to 6
- fine_table: int32 [16384, 6], P('tile'), may hold values from 0 to 16383, as said below
- mid_table: int32 [4096, 6], P('tile'), may hold values from 0 to 4095, as said below
- coarse_table: int32 [1024, 6], replicated, may hold values from 0 to 1023, as said below
- fine_parent: int32 [16384], P('tile'), may hold values from 0 to 4095, as said below
- mid_parent: int32 [4096], P('tile'), may hold values from 0 to 1023, as said below
- edge_self: bfloat16 [3, 512, 512], replicated, may hold values from -0.1875 to 0.1875
- edge_peer: bfloat16 [3, 512, 512], replicated, may hold values from -0.1875 to 0.1875
- edge_bias: float32 [3, 512], replicated, may hold values from -3 to 3
- node_self: bfloat16 [3, 512, 512], replicated, may hold values from -0.1875 to 0.1875
- node_message: bfloat16 [3, 512, 512], replicated, may hold values from -0.109375 to 0.109375
- node_bias: float32 [3, 512], replicated, may hold values from -3 to 3
- node_out: bfloat16 [3, 512, 512], replicated, may hold values from -0.25 to 0.25
- ascend_gain: float32 [2, 512], replicated, may hold values from 0.1 to 1.9
- down_self: bfloat16 [2, 512, 512], replicated, may hold values from -0.1875 to 0.1875
- down_parent: bfloat16 [2, 512, 512], replicated, may hold values from -0.1875 to 0.1875
- down_bias: float32 [2, 512], replicated, may hold values from -3 to 3
- down_out: bfloat16 [2, 512, 512], replicated, may hold values from -0.25 to 0.25
Outputs:
- fine_out: bfloat16 [32768, 512], P(('groups', 'tile')), parts along dimension 0
- mid_out: bfloat16 [8192, 512], P(('groups', 'tile')), parts along dimension 0
- coarse_out: bfloat16 [2048, 512], P(('groups', 'tile')), parts along dimension 0
There are 2 independent parts, one for each index of `groups`. A program takes and returns all parts, laid end to end along the dimension named above; an argument that names none is the same for every part. Nothing has to cross between parts.
Inputs may be any that keep to these rules, and one draw needn't show every extreme that they name: `fine_table`: fine node n is grid cell (n // 256, n % 256); each of its six neighbours lies in its own grid row or one of the two rows beside it, columns wrapping around. `mid_table`: Level-1 node p is cell (p // 128, p % 128); each neighbour lies in its own row or one of the two rows beside it, columns wrapping around. `coarse_table`: any level-2 nodes. `fine_parent`: the parent of fine cell (r, c) lies in level-1 row r // 2 - 1, r // 2 or r // 2 + 1. `mid_parent`: the parent of level-1 cell (r, c) lies in level-2 row r // 2 - 1, r // 2 or r // 2 + 1.
All inputs are finite; a program needn't handle non-finite values.
Results may differ from a plain program's by a relative error of at most 0.014.
Values may be sent and summed in bfloat16 or wider, within the bound.
A program may use at most 64 MiB of HBM per device.

v0:
```python
import jax
import jax.numpy as jnp
from jax import lax
from jax.sharding import PartitionSpec as P

COLS = 256


def with_halo(cells, sides, width):
    for axis, dim in sides:
        count = lax.axis_size(axis)
        ends = count - 1
        head = lax.slice_in_dim(cells, 0, width, axis=dim)
        tail = lax.slice_in_dim(cells, cells.shape[dim] - width, cells.shape[dim], axis=dim)
        cells = jnp.concatenate(
            [
                lax.ppermute(tail, axis, [(i, (i + 1) % count) for i in range(ends)]),
                cells,
                lax.ppermute(head, axis, [((i + 1) % count, i) for i in range(ends)]),
            ],
            axis=dim,
        )
    return cells


def gelu_tanh(values):
    return jax.nn.gelu(values, approximate=True)


def rim_rows(block_rows, col_count):
    feature_count = block_rows.shape[1]
    grid_rows = block_rows.reshape(block_rows.shape[0] // col_count, col_count, feature_count)
    padded = with_halo(grid_rows, (("tile", 0),), 1)
    return padded.reshape(-1, feature_count)


def finish_level(node_rows, summed, level_index, weights):
    node_self = weights[3]
    node_message = weights[4]
    node_bias = weights[5]
    node_out = weights[6]
    message = summed.astype(jnp.bfloat16)
    pre_act = jnp.dot(node_rows, node_self[level_index], preferred_element_type=jnp.float32)
    pre_act = (
        pre_act
        + jnp.dot(message, node_message[level_index], preferred_element_type=jnp.float32)
        + node_bias[level_index]
    )
    hidden = gelu_tanh(pre_act).astype(jnp.bfloat16)
    result = node_rows.astype(jnp.float32) + jnp.dot(
        hidden, node_out[level_index], preferred_element_type=jnp.float32
    )
    return result.astype(jnp.bfloat16)


def own_projection(node_rows, level_index, weights):
    return (
        jnp.dot(node_rows, weights[0][level_index], preferred_element_type=jnp.float32)
        + weights[2][level_index]
    )


def peer_projection(node_rows, level_index, weights):
    return jnp.dot(node_rows, weights[1][level_index], preferred_element_type=jnp.float32).astype(
        jnp.bfloat16
    )


def process_local(node_rows, neighbours, level_index, col_count, weights):
    own_proj = own_projection(node_rows, level_index, weights)
    extended = rim_rows(peer_projection(node_rows, level_index, weights), col_count)
    offset = lax.axis_index("tile") * node_rows.shape[0] - col_count
    local_ids = neighbours - offset
    summed = jnp.zeros(own_proj.shape, jnp.float32)
    for slot_index in range(6):
        fetched = extended[local_ids[:, slot_index]].astype(jnp.float32)
        summed = summed + gelu_tanh(own_proj + fetched)
    return finish_level(node_rows, summed, level_index, weights)


def ascend_local(children, parents, col_up, gain_vec):
    feature_count = children.shape[1]
    rows_up = children.shape[0] // (4 * col_up)
    span_rows = (rows_up + 2) * col_up
    offset = lax.axis_index("tile") * rows_up * col_up - col_up
    local_ids = parents - offset
    onehot = (local_ids[None, :] == jnp.arange(span_rows, dtype=jnp.int32)[:, None]).astype(
        jnp.bfloat16
    )
    partial_value = jnp.dot(onehot, children, preferred_element_type=jnp.float32)
    grid_rows = partial_value.reshape(rows_up + 2, col_up, feature_count)
    padded = with_halo(grid_rows.astype(jnp.bfloat16), (("tile", 0),), 1).astype(grid_rows.dtype)
    summed = grid_rows[1:-1]
    summed = summed.at[0].add(padded[0])
    summed = summed.at[-1].add(padded[-1])
    summed = summed.reshape(rows_up * col_up, feature_count)
    scale_inv = lax.rsqrt(jnp.mean(summed * summed, axis=1, keepdims=True) + 1e-05)
    return (summed * scale_inv * gain_vec).astype(jnp.bfloat16)


def descend_local(children, lifted_ext, parents, col_up, level_index, downs):
    down_self, down_parent, down_bias, down_out = downs
    rows_up = children.shape[0] // (4 * col_up)
    offset = lax.axis_index("tile") * rows_up * col_up - col_up
    fetched = lifted_ext[parents - offset].astype(jnp.float32)
    pre_act = (
        jnp.dot(children, down_self[level_index], preferred_element_type=jnp.float32)
        + fetched
        + down_bias[level_index]
    )
    hidden = gelu_tanh(pre_act).astype(jnp.bfloat16)
    result = children.astype(jnp.float32) + jnp.dot(
        hidden, down_out[level_index], preferred_element_type=jnp.float32
    )
    return result.astype(jnp.bfloat16)


def local(
    fine_nodes,
    fine_table,
    mid_table,
    coarse_table,
    fine_parent,
    mid_parent,
    edge_self,
    edge_peer,
    edge_bias,
    node_self,
    node_message,
    node_bias,
    node_out,
    ascend_gain,
    down_self,
    down_parent,
    down_bias,
    down_out,
):
    weights = (edge_self, edge_peer, edge_bias, node_self, node_message, node_bias, node_out)
    downs = (down_self, down_parent, down_bias, down_out)
    col_mid = COLS // 2
    col_low = COLS // 4
    fine_rows = process_local(fine_nodes, fine_table, 0, COLS, weights)
    mid_start = ascend_local(fine_rows, fine_parent, col_mid, ascend_gain[0])
    mid_rows = process_local(mid_start, mid_table, 1, col_mid, weights)
    coarse_start = ascend_local(mid_rows, mid_parent, col_low, ascend_gain[1])
    coarse_count = coarse_start.shape[0]
    peer_proj = peer_projection(coarse_start, 2, weights)
    own_proj = own_projection(coarse_start, 2, weights)
    my_table = lax.dynamic_slice_in_dim(
        coarse_table, lax.axis_index("tile") * coarse_count, coarse_count, 0
    )
    running = jnp.zeros(own_proj.shape, jnp.float32)
    fragment = lax.all_gather(peer_proj, "tile", axis=0, tiled=True)
    row_count = fragment.shape[0]
    for slot_index in range(6):
        where_ids = my_table[:, slot_index]
        inside = (where_ids >= 0) & (where_ids < row_count)
        fetched = fragment[jnp.clip(where_ids, 0, row_count - 1)].astype(jnp.float32)
        running = running + jnp.where(inside[:, None], gelu_tanh(own_proj + fetched), 0.0)
    coarse_final = finish_level(coarse_start, running, 2, weights)
    lifted_own = jnp.dot(coarse_final, down_parent[1], preferred_element_type=jnp.float32).astype(
        jnp.bfloat16
    )
    lifted_ext = rim_rows(lifted_own, col_low)
    mid_final = descend_local(mid_rows, lifted_ext, mid_parent, col_low, 1, downs)
    lifted_mid = rim_rows(
        jnp.dot(mid_final, down_parent[0], preferred_element_type=jnp.float32).astype(jnp.bfloat16),
        col_mid,
    )
    fine_final = descend_local(fine_rows, lifted_mid, fine_parent, col_mid, 0, downs)
    return (fine_final, mid_final, coarse_final)


def solution(mesh):
    placed = (
        P(("groups", "tile"), None),
        P("tile", None),
        P("tile", None),
        P(),
        P("tile"),
        P("tile"),
        P(),
        P(),
        P(),
        P(),
        P(),
        P(),
        P(),
        P(),
        P(),
        P(),
        P(),
        P(),
    )
    return jax.shard_map(
        local,
        mesh=mesh,
        in_specs=placed,
        out_specs=(
            P(("groups", "tile"), None),
            P(("groups", "tile"), None),
            P(("groups", "tile"), None),
        ),
        check_vma=False,
    )
```

profile of v0, /device:TPU:5, one launch (start us, length us, event | category | flops | bytes accessed | tf_op | source)
XLA Modules:
  0.0 196.6 jit_solution(9857290049073583987)
XLA Ops:
  9.5 3.8 %collective-permute-start = (bf16[1,256,512]{2,1,0:T(8,128)(2,1)S(1)}, bf16[1,256,512]{2,1,0:T(8,128)(2,1)S(1)}, u32[]{:S(2)}, u32[]{:S(2)}) collective-permute-start(bf16[1,256,512]{2,1,0:T(8,128)(2,1)S(1)} %get-tuple-element.57), channel_id=1, source_target_pairs={{0,1},{1,2},{2,3},{3,4},{4,5},{5,6},{6,7},{7,8},{8,9},{9,10},{10,1... | collective-permute-start | bytes 786440 | tf_op jit(solution)/shard_map/ppermute | solution.py:17
  15.5 3.1 %fusion.175 = f32[1024,512]{1,0:T(8,128)} fusion(bf16[1024,512]{1,0:T(8,128)(2,1)S(1)} %copy-done.3, bf16[3,512,512]{2,1,0:T(8,128)(2,1)} %param.35), kind=kOutput, calls=%fused_computation.221 | convolution fusion | flops 536870912 | bytes 3670016 | tf_op jit(solution)/shard_map/dot_general | solution.py:43
  18.7 3.2 %collective-permute-done.1 = bf16[1,256,512]{2,1,0:T(8,128)(2,1)S(1)} collective-permute-done((bf16[1,256,512]{2,1,0:T(8,128)(2,1)S(1)}, bf16[1,256,512]{2,1,0:T(8,128)(2,1)S(1)}, u32[]{:S(2)}, u32[]{:S(2)}) %collective-permute-start.1) | collective-permute-done | bytes 262176 | tf_op jit(solution)/shard_map/ppermute | solution.py:19
  22.1 5.1 %gather_fusion = bf16[1024,512]{1,0:T(8,128)(2,1)} fusion(bf16[1536,512]{1,0:T(8,128)(2,1)S(1)} %bitcast.201, s32[1024]{0:T(1024)S(1)} %broadcast_clamp_fusion.5), kind=kCustom, calls=%fused_computation | custom fusion | bytes 2101248 | tf_op jit(solution)/shard_map/gather | solution.py:76
  27.2 5.1 %gather_fusion.1 = bf16[1024,512]{1,0:T(8,128)(2,1)} fusion(bf16[1536,512]{1,0:T(8,128)(2,1)S(1)} %bitcast.202, s32[1024]{0:T(1024)S(1)} %broadcast_clamp_fusion.4), kind=kCustom, calls=%fused_computation.1 | custom fusion | bytes 2101248 | tf_op jit(solution)/shard_map/gather | solution.py:76
  32.3 5.1 %gather_fusion.2 = bf16[1024,512]{1,0:T(8,128)(2,1)} fusion(bf16[1536,512]{1,0:T(8,128)(2,1)S(1)} %bitcast.203, s32[1024]{0:T(1024)S(1)} %broadcast_clamp_fusion.3), kind=kCustom, calls=%fused_computation.2 | custom fusion | bytes 2101248 | tf_op jit(solution)/shard_map/gather | solution.py:76
  37.4 5.0 %gather_fusion.3 = bf16[1024,512]{1,0:T(8,128)(2,1)} fusion(bf16[1536,512]{1,0:T(8,128)(2,1)S(1)} %bitcast.204, s32[1024]{0:T(1024)S(1)} %broadcast_clamp_fusion.2), kind=kCustom, calls=%fused_computation.3 | custom fusion | bytes 2101248 | tf_op jit(solution)/shard_map/gather | solution.py:76
  42.4 5.1 %gather_fusion.4 = bf16[1024,512]{1,0:T(8,128)(2,1)} fusion(bf16[1536,512]{1,0:T(8,128)(2,1)S(1)} %bitcast.205, s32[1024]{0:T(1024)S(1)} %broadcast_clamp_fusion.1), kind=kCustom, calls=%fused_computation.4 | custom fusion | bytes 2101248 | tf_op jit(solution)/shard_map/gather | solution.py:76
  47.5 5.1 %gather_fusion.5 = bf16[1024,512]{1,0:T(8,128)(2,1)} fusion(bf16[1536,512]{1,0:T(8,128)(2,1)S(1)} %bitcast.206, s32[1024]{0:T(1024)S(1)} %broadcast_clamp_fusion), kind=kCustom, calls=%fused_computation.5 | custom fusion | bytes 2101248 | tf_op jit(solution)/shard_map/gather | solution.py:76
  52.5 10.0 %fusion.54 = bf16[1024,512]{1,0:T(8,128)(2,1)S(1)} fusion(f32[1024,512]{1,0:T(8,128)} %fusion.175, f32[512]{0:T(512)S(1)} %bitcast.245, bf16[1024,512]{1,0:T(8,128)(2,1)} %gather_fusion.5, bf16[1024,512]{1,0:T(8,128)(2,1)} %gather_fusion.4, bf16[1024,512]{1,0:T(8,128)(2,1)} %gather_fusion.3, bf16[1024,512]{1,0:T(8,128)(2,1)} %gather_fusion.2, ...), kind=kOutput, calls=%fused_computation.82 | convolution fusion | flops 1114636288 | bytes 11538432 | tf_op jit(solution)/shard_map/dot_general | solution.py:46
  67.0 2.6 %collective-permute-start.3 = (bf16[1,128,512]{2,1,0:T(8,128)(2,1)S(1)}, bf16[1,128,512]{2,1,0:T(8,128)(2,1)S(1)}, u32[]{:S(2)}, u32[]{:S(2)}) collective-permute-start(bf16[1,128,512]{2,1,0:T(8,128)(2,1)S(1)} %get-tuple-element.60), channel_id=1, source_target_pairs={{1,0},{2,1},{3,2},{4,3},{5,4},{6,5},{7,6},{8,7},{9,8},{10,9},{11,1... | collective-permute-start | bytes 393224 | tf_op jit(solution)/shard_map/ppermute | solution.py:19
  69.7 4.5 %collective-permute-done.3 = bf16[1,128,512]{2,1,0:T(8,128)(2,1)S(1)} collective-permute-done((bf16[1,128,512]{2,1,0:T(8,128)(2,1)S(1)}, bf16[1,128,512]{2,1,0:T(8,128)(2,1)S(1)}, u32[]{:S(2)}, u32[]{:S(2)}) %collective-permute-start.3) | collective-permute-done | bytes 131104 | tf_op jit(solution)/shard_map/ppermute | solution.py:19
  78.3 2.4 %collective-permute-start.5 = (bf16[1,128,512]{2,1,0:T(8,128)(2,1)S(1)}, bf16[1,128,512]{2,1,0:T(8,128)(2,1)S(1)}, u32[]{:S(2)}, u32[]{:S(2)}) collective-permute-start(bf16[1,128,512]{2,1,0:T(8,128)(2,1)S(1)} %get-tuple-element.64), channel_id=1, source_target_pairs={{1,0},{2,1},{3,2},{4,3},{5,4},{6,5},{7,6},{8,7},{9,8},{10,9},{11,1... | collective-permute-start | bytes 393224 | tf_op jit(solution)/shard_map/ppermute | solution.py:19
  82.9 2.6 %collective-permute-done.5 = bf16[1,128,512]{2,1,0:T(8,128)(2,1)S(1)} collective-permute-done((bf16[1,128,512]{2,1,0:T(8,128)(2,1)S(1)}, bf16[1,128,512]{2,1,0:T(8,128)(2,1)S(1)}, u32[]{:S(2)}, u32[]{:S(2)}) %collective-permute-start.5) | collective-permute-done | bytes 131104 | tf_op jit(solution)/shard_map/ppermute | solution.py:19
  96.0 3.3 %fusion.66 = bf16[256,512]{1,0:T(8,128)(2,1)S(1)} fusion(f32[256,512]{1,0:T(8,128)S(1)} %fusion.160, bf16[3,512,512]{2,1,0:T(8,128)(2,1)} %param.38, bf16[3,512,512]{2,1,0:T(8,128)(2,1)} %param.36, bf16[256,512]{1,0:T(8,128)(2,1)} %fusion.163, f32[256,512]{1,0:T(8,128)S(1)} %convolution_add_fusion.3, bf16[256,512]{1,0:T(8,128)(2,1)} %gather_fusion.11, ...), kind=kOutput, calls=%fused_computation.103 | convolution fusion | flops 278921216 | bytes 4196352 | tf_op jit(solution)/shard_map/dot_general | solution.py:50
  101.5 2.4 %collective-permute-start.7 = (bf16[1,64,512]{2,1,0:T(8,128)(2,1)S(1)}, bf16[1,64,512]{2,1,0:T(8,128)(2,1)S(1)}, u32[]{:S(2)}, u32[]{:S(2)}) collective-permute-start(bf16[1,64,512]{2,1,0:T(8,128)(2,1)S(1)} %get-tuple-element.66), channel_id=1, source_target_pairs={{1,0},{2,1},{3,2},{4,3},{5,4},{6,5},{7,6},{8,7},{9,8},{10,9},{11,1... | collective-permute-start | bytes 196616 | tf_op jit(solution)/shard_map/ppermute | solution.py:19
  103.9 4.1 %collective-permute-done.7 = bf16[1,64,512]{2,1,0:T(8,128)(2,1)S(1)} collective-permute-done((bf16[1,64,512]{2,1,0:T(8,128)(2,1)S(1)}, bf16[1,64,512]{2,1,0:T(8,128)(2,1)S(1)}, u32[]{:S(2)}, u32[]{:S(2)}) %collective-permute-start.7) | collective-permute-done | bytes 65568 | tf_op jit(solution)/shard_map/ppermute | solution.py:19
  110.5 36.7 %all-gather.2.cloned.1.call-done = bf16[1024,512]{1,0:T(8,128)(2,1)} async-done(((bf16[64,512]{1,0:T(8,128)(2,1)}), bf16[1024,512]{1,0:T(8,128)(2,1)}) %all-gather.2.cloned.1.call-update) | async-done | bytes 1048592 | tf_op jit(solution)/shard_map/all_gather | solution.py:153
  159.1 3.4 %collective-permute-start.8 = (bf16[1,64,512]{2,1,0:T(8,128)(2,1)S(1)}, bf16[1,64,512]{2,1,0:T(8,128)(2,1)S(1)}, u32[]{:S(2)}, u32[]{:S(2)}) collective-permute-start(bf16[1,64,512]{2,1,0:T(8,128)(2,1)S(1)} %fusion.70), channel_id=1, source_target_pairs={{0,1},{1,2},{2,3},{3,4},{4,5},{5,6},{6,7},{7,8},{8,9},{9,10},{10,1... | collective-permute-start | bytes 196616 | tf_op jit(solution)/shard_map/ppermute | solution.py:17
  164.5 4.5 %collective-permute-done.9 = bf16[1,64,512]{2,1,0:T(8,128)(2,1)S(1)} collective-permute-done((bf16[1,64,512]{2,1,0:T(8,128)(2,1)S(1)}, bf16[1,64,512]{2,1,0:T(8,128)(2,1)S(1)}, u32[]{:S(2)}, u32[]{:S(2)}) %collective-permute-start.9) | collective-permute-done | bytes 65568 | tf_op jit(solution)/shard_map/ppermute | solution.py:19
  174.2 2.4 %collective-permute-start.11 = (bf16[1,128,512]{2,1,0:T(8,128)(2,1)S(1)}, bf16[1,128,512]{2,1,0:T(8,128)(2,1)S(1)}, u32[]{:S(2)}, u32[]{:S(2)}) collective-permute-start(bf16[1,128,512]{2,1,0:T(8,128)(2,1)S(1)} %get-tuple-element.62), channel_id=1, source_target_pairs={{1,0},{2,1},{3,2},{4,3},{5,4},{6,5},{7,6},{8,7},{9,8},{10,9},{11,1... | collective-permute-start | bytes 393224 | tf_op jit(solution)/shard_map/ppermute | solution.py:19
  176.6 4.8 %collective-permute-done.11 = bf16[1,128,512]{2,1,0:T(8,128)(2,1)S(1)} collective-permute-done((bf16[1,128,512]{2,1,0:T(8,128)(2,1)S(1)}, bf16[1,128,512]{2,1,0:T(8,128)(2,1)S(1)}, u32[]{:S(2)}, u32[]{:S(2)}) %collective-permute-start.11) | collective-permute-done | bytes 131104 | tf_op jit(solution)/shard_map/ppermute | solution.py:19
  181.4 4.0 %gather_fusion.19 = bf16[1024,512]{1,0:T(8,128)(2,1)S(1)} fusion(bf16[512,512]{1,0:T(8,128)(2,1)S(1)} %bitcast.213, s32[1024]{0:T(1024)S(1)} %get-tuple-element.51), kind=kCustom, calls=%fused_computation.19 | custom fusion | bytes 2101248 | tf_op jit(solution)/shard_map/gather | solution.py:105
  185.4 4.3 %add_convert_fusion = bf16[1024,512]{1,0:T(8,128)(2,1)} fusion(bf16[1024,512]{1,0:T(8,128)(2,1)} %copy-done.17, bf16[1024,512]{1,0:T(8,128)(2,1)S(1)} %gather_fusion.19, f32[512]{0:T(512)S(1)} %bitcast.244, bf16[2,512,512]{2,1,0:T(8,128)(2,1)S(1)} %copy-done.15, bf16[2,512,512]{2,1,0:T(8,128)(2,1)} %param.40), kind=kOutput, calls=%fused_computation.91 | convolution fusion | flops 1081606144 | bytes 5244928 | tf_op jit(solution)/shard_map/dot_general | solution.py:112
  (125 shorter events, 49.3 us)
Async XLA Ops:
  7.2 102.9 %copy-start = (s32[1024,6]{0,1:T(8,128)S(1)}, s32[1024,6]{0,1:T(8,128)}, u32[]{:S(2)}) copy-start(s32[1024,6]{0,1:T(8,128)} %param.29) | copy-start | bytes 73732
  7.2 8.3 %copy-start.3 = (bf16[1024,512]{1,0:T(8,128)(2,1)S(1)}, bf16[1024,512]{1,0:T(8,128)(2,1)}, u32[]{:S(2)}) copy-start(bf16[1024,512]{1,0:T(8,128)(2,1)} %param.26) | copy-start | bytes 3145732
  7.2 139.9 %all-gather.2.cloned.1.call-start = ((), (), s32[]{:S(2)}) async-start(), calls=%async_computation | async-start | bytes 1114112 | tf_op jit(solution)/shard_map/all_gather | solution.py:153
  9.4 9.1 %copy-start.12 = (f32[2,512]{1,0:T(2,128)S(1)}, f32[2,512]{1,0:T(2,128)}, u32[]{:S(2)}) copy-start(f32[2,512]{1,0:T(2,128)} %param.39) | copy-start | bytes 12292
  9.5 9.1 %copy-start.11 = (s32[1024]{0:T(1024)S(1)}, s32[1024]{0:T(1024)}, u32[]{:S(2)}) copy-start(s32[1024]{0:T(1024)} %param.30) | copy-start | bytes 12292
  9.5 9.1 %copy-start.8 = (s32[256,6]{0,1:T(8,128)S(1)}, s32[256,6]{0,1:T(8,128)}, u32[]{:S(2)}) copy-start(s32[256,6]{0,1:T(8,128)} %param.28) | copy-start | bytes 18436
  9.5 9.2 %copy-start.14 = (s32[256]{0:T(256)S(1)}, s32[256]{0:T(256)}, u32[]{:S(2)}) copy-start(s32[256]{0:T(256)} %param.31) | copy-start | bytes 3076
  9.5 9.2 %copy-start.10 = (f32[3,512]{1,0:T(4,128)S(1)}, f32[3,512]{1,0:T(4,128)}, u32[]{:S(2)}) copy-start(f32[3,512]{1,0:T(4,128)} %param.34) | copy-start | bytes 18436
  9.5 9.2 %collective-permute-start = (bf16[1,256,512]{2,1,0:T(8,128)(2,1)S(1)}, bf16[1,256,512]{2,1,0:T(8,128)(2,1)S(1)}, u32[]{:S(2)}, u32[]{:S(2)}) collective-permute-start(bf16[1,256,512]{2,1,0:T(8,128)(2,1)S(1)} %get-tuple-element.57), channel_id=1, source_target_pairs={{0,1},{1,2},{2,3},{3,4},{4,5},{5,6},{6,7},{7,8},{8,9},{9,10},{10,1... | collective-permute-start | bytes 786440 | tf_op jit(solution)/shard_map/ppermute | solution.py:17
  13.4 8.6 %collective-permute-start.1 = (bf16[1,256,512]{2,1,0:T(8,128)(2,1)S(1)}, bf16[1,256,512]{2,1,0:T(8,128)(2,1)S(1)}, u32[]{:S(2)}, u32[]{:S(2)}) collective-permute-start(bf16[1,256,512]{2,1,0:T(8,128)(2,1)S(1)} %get-tuple-element.58), channel_id=1, source_target_pairs={{1,0},{2,1},{3,2},{4,3},{5,4},{6,5},{7,6},{8,7},{9,8},{10,9},{11,1... | collective-permute-start | bytes 786440 | tf_op jit(solution)/shard_map/ppermute | solution.py:19
  65.1 4.6 %collective-permute-start.2 = (bf16[1,128,512]{2,1,0:T(8,128)(2,1)S(1)}, bf16[1,128,512]{2,1,0:T(8,128)(2,1)S(1)}, u32[]{:S(2)}, u32[]{:S(2)}) collective-permute-start(bf16[1,128,512]{2,1,0:T(8,128)(2,1)S(1)} %get-tuple-element.59), channel_id=1, source_target_pairs={{0,1},{1,2},{2,3},{3,4},{4,5},{5,6},{6,7},{7,8},{8,9},{9,10},{10,1... | collective-permute-start | bytes 393224 | tf_op jit(solution)/shard_map/ppermute | solution.py:17
  67.0 7.2 %collective-permute-start.3 = (bf16[1,128,512]{2,1,0:T(8,128)(2,1)S(1)}, bf16[1,128,512]{2,1,0:T(8,128)(2,1)S(1)}, u32[]{:S(2)}, u32[]{:S(2)}) collective-permute-start(bf16[1,128,512]{2,1,0:T(8,128)(2,1)S(1)} %get-tuple-element.60), channel_id=1, source_target_pairs={{1,0},{2,1},{3,2},{4,3},{5,4},{6,5},{7,6},{8,7},{9,8},{10,9},{11,1... | collective-permute-start | bytes 393224 | tf_op jit(solution)/shard_map/ppermute | solution.py:19
  76.4 6.5 %collective-permute-start.4 = (bf16[1,128,512]{2,1,0:T(8,128)(2,1)S(1)}, bf16[1,128,512]{2,1,0:T(8,128)(2,1)S(1)}, u32[]{:S(2)}, u32[]{:S(2)}) collective-permute-start(bf16[1,128,512]{2,1,0:T(8,128)(2,1)S(1)} %get-tuple-element.63), channel_id=1, source_target_pairs={{0,1},{1,2},{2,3},{3,4},{4,5},{5,6},{6,7},{7,8},{8,9},{9,10},{10,1... | collective-permute-start | bytes 393224 | tf_op jit(solution)/shard_map/ppermute | solution.py:17
  78.3 7.2 %collective-permute-start.5 = (bf16[1,128,512]{2,1,0:T(8,128)(2,1)S(1)}, bf16[1,128,512]{2,1,0:T(8,128)(2,1)S(1)}, u32[]{:S(2)}, u32[]{:S(2)}) collective-permute-start(bf16[1,128,512]{2,1,0:T(8,128)(2,1)S(1)} %get-tuple-element.64), channel_id=1, source_target_pairs={{1,0},{2,1},{3,2},{4,3},{5,4},{6,5},{7,6},{8,7},{9,8},{10,9},{11,1... | collective-permute-start | bytes 393224 | tf_op jit(solution)/shard_map/ppermute | solution.py:19
  99.3 11.0 %copy-start.13 = (f32[2,512]{1,0:T(2,128)S(1)}, f32[2,512]{1,0:T(2,128)}, u32[]{:S(2)}) copy-start(f32[2,512]{1,0:T(2,128)} %param.42) | copy-start | bytes 12292
  99.5 4.3 %collective-permute-start.6 = (bf16[1,64,512]{2,1,0:T(8,128)(2,1)S(1)}, bf16[1,64,512]{2,1,0:T(8,128)(2,1)S(1)}, u32[]{:S(2)}, u32[]{:S(2)}) collective-permute-start(bf16[1,64,512]{2,1,0:T(8,128)(2,1)S(1)} %get-tuple-element.65), channel_id=1, source_target_pairs={{0,1},{1,2},{2,3},{3,4},{4,5},{5,6},{6,7},{7,8},{8,9},{9,10},{10,1... | collective-permute-start | bytes 196616 | tf_op jit(solution)/shard_map/ppermute | solution.py:17
  101.5 6.5 %collective-permute-start.7 = (bf16[1,64,512]{2,1,0:T(8,128)(2,1)S(1)}, bf16[1,64,512]{2,1,0:T(8,128)(2,1)S(1)}, u32[]{:S(2)}, u32[]{:S(2)}) collective-permute-start(bf16[1,64,512]{2,1,0:T(8,128)(2,1)S(1)} %get-tuple-element.66), channel_id=1, source_target_pairs={{1,0},{2,1},{3,2},{4,3},{5,4},{6,5},{7,6},{8,7},{9,8},{10,9},{11,1... | collective-permute-start | bytes 196616 | tf_op jit(solution)/shard_map/ppermute | solution.py:19
  158.9 13.0 %copy-start.6 = (bf16[64,512]{1,0:T(8,128)(2,1)}, bf16[64,512]{1,0:T(8,128)(2,1)S(1)}, u32[]{:S(2)}) copy-start(bf16[64,512]{1,0:T(8,128)(2,1)S(1)} %fusion.69) | copy-start | bytes 196612
  158.9 11.3 %copy-start.15 = (bf16[2,512,512]{2,1,0:T(8,128)(2,1)S(1)}, bf16[2,512,512]{2,1,0:T(8,128)(2,1)}, u32[]{:S(2)}) copy-start(bf16[2,512,512]{2,1,0:T(8,128)(2,1)} %param.43) | copy-start | bytes 3145732
  159.1 5.4 %collective-permute-start.8 = (bf16[1,64,512]{2,1,0:T(8,128)(2,1)S(1)}, bf16[1,64,512]{2,1,0:T(8,128)(2,1)S(1)}, u32[]{:S(2)}, u32[]{:S(2)}) collective-permute-start(bf16[1,64,512]{2,1,0:T(8,128)(2,1)S(1)} %fusion.70), channel_id=1, source_target_pairs={{0,1},{1,2},{2,3},{3,4},{4,5},{5,6},{6,7},{7,8},{8,9},{9,10},{10,1... | collective-permute-start | bytes 196616 | tf_op jit(solution)/shard_map/ppermute | solution.py:17
  162.6 6.5 %collective-permute-start.9 = (bf16[1,64,512]{2,1,0:T(8,128)(2,1)S(1)}, bf16[1,64,512]{2,1,0:T(8,128)(2,1)S(1)}, u32[]{:S(2)}, u32[]{:S(2)}) collective-permute-start(bf16[1,64,512]{2,1,0:T(8,128)(2,1)S(1)} %fusion.70), channel_id=1, source_target_pairs={{1,0},{2,1},{3,2},{4,3},{5,4},{6,5},{7,6},{8,7},{9,8},{10,9},{11,1... | collective-permute-start | bytes 196616 | tf_op jit(solution)/shard_map/ppermute | solution.py:19
  171.9 13.5 %copy-start.16 = (bf16[256,512]{1,0:T(8,128)(2,1)}, bf16[256,512]{1,0:T(8,128)(2,1)S(1)}, u32[]{:S(2)}) copy-start(bf16[256,512]{1,0:T(8,128)(2,1)S(1)} %fusion.67) | copy-start | bytes 786436
  172.3 4.3 %collective-permute-start.10 = (bf16[1,128,512]{2,1,0:T(8,128)(2,1)S(1)}, bf16[1,128,512]{2,1,0:T(8,128)(2,1)S(1)}, u32[]{:S(2)}, u32[]{:S(2)}) collective-permute-start(bf16[1,128,512]{2,1,0:T(8,128)(2,1)S(1)} %get-tuple-element.61), channel_id=1, source_target_pairs={{0,1},{1,2},{2,3},{3,4},{4,5},{5,6},{6,7},{7,8},{8,9},{9,10},{10,1... | collective-permute-start | bytes 393224 | tf_op jit(solution)/shard_map/ppermute | solution.py:17
  174.2 7.2 %collective-permute-start.11 = (bf16[1,128,512]{2,1,0:T(8,128)(2,1)S(1)}, bf16[1,128,512]{2,1,0:T(8,128)(2,1)S(1)}, u32[]{:S(2)}, u32[]{:S(2)}) collective-permute-start(bf16[1,128,512]{2,1,0:T(8,128)(2,1)S(1)} %get-tuple-element.62), channel_id=1, source_target_pairs={{1,0},{2,1},{3,2},{4,3},{5,4},{6,5},{7,6},{8,7},{9,8},{10,9},{11,1... | collective-permute-start | bytes 393224 | tf_op jit(solution)/shard_map/ppermute | solution.py:19
  (7 other events, 38.2 us)
Sparse Core Ops, SparseCore 0:
  110.2 36.9 all-gather.1
where the time goes:
time: 198 us; the launch traced here: 197 us
  waiting for transfers between devices  60.4 us (31%)
  local copies, waits for them, and re-layouts  54.7 us (28%)
  matrix products  36.1 us (18%)
  starting transfers between devices  28.6 us (14%)
  between operations  14.9 us (8%)
    gather x12, local copies, waits for them, and re-layouts, process_local(): fetched = extended[local_ids[:, slot_index]].astype(jnp.float32)  40.9 us
    all_gather x1, waiting for transfers between devices, local(): fragment = lax.all_gather(peer_proj, 'tile', axis=0, tiled=True)  36.7 us
    ppermute x6, waiting for transfers between devices, with_halo(): lax.ppermute(head, axis, [((i + 1) % count, i) for i in range(ends)])  23.7 us
    ppermute x6, starting transfers between devices, with_halo(): lax.ppermute(tail, axis, [(i, (i + 1) % count) for i in range(ends)])  14.9 us
    ppermute x6, starting transfers between devices, with_halo(): lax.ppermute(head, axis, [((i + 1) % count, i) for i in range(ends)])  13.6 us
    dot_general x1, matrix products, finish_level(): jnp.dot(message, node_message[level_index], preferred_element_type=jnp.fl...  9.98 us
    gather x6, local copies, waits for them, and re-layouts, local(): fragment[jnp.clip(where_ids, 0, row_count - 1)].astype(jnp.float32)  8.41 us
    dot_general x3, matrix products, finish_level(): jnp.dot(hidden, node_out[level_index], preferred_element_type=jnp.float32)  6.61 us
  transfers between devices with their start and end apart: 13, of which 7 were waited for; matrix products, arithmetic and copies ran while one was open for 3% of the time, Pallas kernels for 0%

commit v1 on v0

--- a/solution.py
+++ b/solution.py
@@ -150,7 +150,16 @@
         coarse_table, lax.axis_index("tile") * coarse_count, coarse_count, 0
     )
     running = jnp.zeros(own_proj.shape, jnp.float32)
-    fragment = lax.all_gather(peer_proj, "tile", axis=0, tiled=True)
+    before = lax.axis_size("tile")
+    piece_now = lax.axis_index("tile")
+    val2, u1 = (before, piece_now)
+    fragment, low = (peer_proj, 1)
+    while low < val2:
+        reply = lax.ppermute(fragment, "tile", [(j0, j0 ^ low) for j0 in range(val2)])
+        r2 = jnp.concatenate([fragment, reply], axis=0)
+        local_part = jnp.concatenate([reply, fragment], axis=0)
+        fragment = jnp.where(u1 & low == 0, r2, local_part)
+        low = 2 * low
     row_count = fragment.shape[0]
     for slot_index in range(6):
         where_ids = my_table[:, slot_index]

time: 198 us -> 180 us (0.909)
  between operations: 14.9 us -> 1.52 us
  waiting for transfers between devices: 60.4 us -> 55.8 us
  local copies, waits for them, and re-layouts: 54.7 us -> 50.7 us
  starting transfers between devices: 28.6 us -> 32.6 us
    all_gather x1 -> x0, waiting for transfers between devices: 36.7 us -> none  [local(): fragment = lax.all_gather(peer_proj, 'tile', axis=0, tiled=True)]
    ppermute x0 -> x4, waiting for transfers between devices: none -> 32.8 us  [local(): lax.ppermute(fragment, 'tile', [(j0, j0 ^ low) for j0 in range(val2)])]
    gather x6, local copies, waits for them, and re-layouts: 8.41 us -> 4.21 us  [local(): fragment[jnp.clip(where_ids, 0, row_count - 1)].astype(jnp.float32)]
    ppermute x0 -> x4, starting transfers between devices: none -> 3.88 us  [local(): lax.ppermute(fragment, 'tile', [(j0, j0 ^ low) for j0 in range(val2)])]
  transfers between devices with their start and end apart: 13 -> 16, of which waited for: 7 -> 10; matrix products, arithmetic and copies ran while one was open for 3% -> 4% of each run, Pallas kernels for 0% -> 0%
where the time goes in v1:
time: 180 us; the launch traced here: 179 us
  waiting for transfers between devices  55.8 us (31%)
  local copies, waits for them, and re-layouts  50.7 us (28%)
  matrix products  35.4 us (20%)
  starting transfers between devices  32.6 us (18%)
  other arithmetic  2.63 us (1%)
    gather x12, local copies, waits for them, and re-layouts, process_local(): fetched = extended[local_ids[:, slot_index]].astype(jnp.float32)  40.8 us
    ppermute x4, waiting for transfers between devices, local(): lax.ppermute(fragment, 'tile', [(j0, j0 ^ low) for j0 in range(val2)])  32.8 us
    ppermute x6, waiting for transfers between devices, with_halo(): lax.ppermute(head, axis, [((i + 1) % count, i) for i in range(ends)])  23 us
    ppermute x6, starting transfers between devices, with_halo(): lax.ppermute(tail, axis, [(i, (i + 1) % count) for i in range(ends)])  14.4 us
    ppermute x6, starting transfers between devices, with_halo(): lax.ppermute(head, axis, [((i + 1) % count, i) for i in range(ends)])  14.3 us
    dot_general x1, matrix products, finish_level(): jnp.dot(message, node_message[level_index], preferred_element_type=jnp.fl...  9.97 us
    dot_general x3, matrix products, finish_level(): jnp.dot(hidden, node_out[level_index], preferred_element_type=jnp.float32)  6.99 us
    dot_general x2, matrix products, descend_local(): jnp.dot(hidden, down_out[level_index], preferred_element_type=jnp.float32)  6.01 us
  transfers between devices with their start and end apart: 16, of which 10 were waited for; matrix products, arithmetic and copies ran while one was open for 4% of the time, Pallas kernels for 0%

profile of v1, /device:TPU:5, one launch (start us, length us, event | category | flops | bytes accessed | tf_op | source)
XLA Modules:
  0.0 178.6 jit_solution(2586097436608066798)
XLA Ops:
  2.9 3.8 %collective-permute-start = (bf16[1,256,512]{2,1,0:T(8,128)(2,1)S(1)}, bf16[1,256,512]{2,1,0:T(8,128)(2,1)S(1)}, u32[]{:S(2)}, u32[]{:S(2)}) collective-permute-start(bf16[1,256,512]{2,1,0:T(8,128)(2,1)S(1)} %get-tuple-element.57), channel_id=1, source_target_pairs={{0,1},{1,2},{2,3},{3,4},{4,5},{5,6},{6,7},{7,8},{8,9},{9,10},{10,1... | collective-permute-start | bytes 786440 | tf_op jit(solution)/shard_map/ppermute | solution.py:17
  8.9 3.1 %fusion.175 = f32[1024,512]{1,0:T(8,128)} fusion(bf16[1024,512]{1,0:T(8,128)(2,1)S(1)} %copy-done.2, bf16[3,512,512]{2,1,0:T(8,128)(2,1)} %param.35), kind=kOutput, calls=%fused_computation.223 | convolution fusion | flops 536870912 | bytes 3670016 | tf_op jit(solution)/shard_map/dot_general | solution.py:43
  12.2 3.2 %collective-permute-done.1 = bf16[1,256,512]{2,1,0:T(8,128)(2,1)S(1)} collective-permute-done((bf16[1,256,512]{2,1,0:T(8,128)(2,1)S(1)}, bf16[1,256,512]{2,1,0:T(8,128)(2,1)S(1)}, u32[]{:S(2)}, u32[]{:S(2)}) %collective-permute-start.1) | collective-permute-done | bytes 262176 | tf_op jit(solution)/shard_map/ppermute | solution.py:19
  15.6 5.1 %gather_fusion = bf16[1024,512]{1,0:T(8,128)(2,1)} fusion(bf16[1536,512]{1,0:T(8,128)(2,1)S(1)} %bitcast.196, s32[1024]{0:T(1024)S(1)} %broadcast_clamp_fusion.5), kind=kCustom, calls=%fused_computation | custom fusion | bytes 2101248 | tf_op jit(solution)/shard_map/gather | solution.py:76
  20.6 5.0 %gather_fusion.1 = bf16[1024,512]{1,0:T(8,128)(2,1)} fusion(bf16[1536,512]{1,0:T(8,128)(2,1)S(1)} %bitcast.197, s32[1024]{0:T(1024)S(1)} %broadcast_clamp_fusion.4), kind=kCustom, calls=%fused_computation.1 | custom fusion | bytes 2101248 | tf_op jit(solution)/shard_map/gather | solution.py:76
  25.7 5.1 %gather_fusion.2 = bf16[1024,512]{1,0:T(8,128)(2,1)} fusion(bf16[1536,512]{1,0:T(8,128)(2,1)S(1)} %bitcast.198, s32[1024]{0:T(1024)S(1)} %broadcast_clamp_fusion.3), kind=kCustom, calls=%fused_computation.2 | custom fusion | bytes 2101248 | tf_op jit(solution)/shard_map/gather | solution.py:76
  30.7 5.1 %gather_fusion.3 = bf16[1024,512]{1,0:T(8,128)(2,1)} fusion(bf16[1536,512]{1,0:T(8,128)(2,1)S(1)} %bitcast.199, s32[1024]{0:T(1024)S(1)} %broadcast_clamp_fusion.2), kind=kCustom, calls=%fused_computation.3 | custom fusion | bytes 2101248 | tf_op jit(solution)/shard_map/gather | solution.py:76
  35.8 5.1 %gather_fusion.4 = bf16[1024,512]{1,0:T(8,128)(2,1)} fusion(bf16[1536,512]{1,0:T(8,128)(2,1)S(1)} %bitcast.200, s32[1024]{0:T(1024)S(1)} %broadcast_clamp_fusion.1), kind=kCustom, calls=%fused_computation.4 | custom fusion | bytes 2101248 | tf_op jit(solution)/shard_map/gather | solution.py:76
  40.8 5.1 %gather_fusion.5 = bf16[1024,512]{1,0:T(8,128)(2,1)} fusion(bf16[1536,512]{1,0:T(8,128)(2,1)S(1)} %bitcast.201, s32[1024]{0:T(1024)S(1)} %broadcast_clamp_fusion), kind=kCustom, calls=%fused_computation.5 | custom fusion | bytes 2101248 | tf_op jit(solution)/shard_map/gather | solution.py:76
  45.9 10.0 %fusion.54 = bf16[1024,512]{1,0:T(8,128)(2,1)S(1)} fusion(f32[1024,512]{1,0:T(8,128)} %fusion.175, f32[512]{0:T(512)S(1)} %bitcast.241, bf16[1024,512]{1,0:T(8,128)(2,1)} %gather_fusion.5, bf16[1024,512]{1,0:T(8,128)(2,1)} %gather_fusion.4, bf16[1024,512]{1,0:T(8,128)(2,1)} %gather_fusion.3, bf16[1024,512]{1,0:T(8,128)(2,1)} %gather_fusion.2, ...), kind=kOutput, calls=%fused_computation.82 | convolution fusion | flops 1114636288 | bytes 11538432 | tf_op jit(solution)/shard_map/dot_general | solution.py:46
  60.6 2.6 %collective-permute-start.3 = (bf16[1,128,512]{2,1,0:T(8,128)(2,1)S(1)}, bf16[1,128,512]{2,1,0:T(8,128)(2,1)S(1)}, u32[]{:S(2)}, u32[]{:S(2)}) collective-permute-start(bf16[1,128,512]{2,1,0:T(8,128)(2,1)S(1)} %get-tuple-element.60), channel_id=1, source_target_pairs={{1,0},{2,1},{3,2},{4,3},{5,4},{6,5},{7,6},{8,7},{9,8},{10,9},{11,1... | collective-permute-start | bytes 393224 | tf_op jit(solution)/shard_map/ppermute | solution.py:19
  63.2 4.5 %collective-permute-done.3 = bf16[1,128,512]{2,1,0:T(8,128)(2,1)S(1)} collective-permute-done((bf16[1,128,512]{2,1,0:T(8,128)(2,1)S(1)}, bf16[1,128,512]{2,1,0:T(8,128)(2,1)S(1)}, u32[]{:S(2)}, u32[]{:S(2)}) %collective-permute-start.3) | collective-permute-done | bytes 131104 | tf_op jit(solution)/shard_map/ppermute | solution.py:19
  76.4 2.6 %collective-permute-done.5 = bf16[1,128,512]{2,1,0:T(8,128)(2,1)S(1)} collective-permute-done((bf16[1,128,512]{2,1,0:T(8,128)(2,1)S(1)}, bf16[1,128,512]{2,1,0:T(8,128)(2,1)S(1)}, u32[]{:S(2)}, u32[]{:S(2)}) %collective-permute-start.5) | collective-permute-done | bytes 131104 | tf_op jit(solution)/shard_map/ppermute | solution.py:19
  89.5 3.3 %fusion.66 = bf16[256,512]{1,0:T(8,128)(2,1)S(1)} fusion(f32[256,512]{1,0:T(8,128)S(1)} %fusion.160, bf16[3,512,512]{2,1,0:T(8,128)(2,1)} %param.38, bf16[3,512,512]{2,1,0:T(8,128)(2,1)} %param.36, bf16[256,512]{1,0:T(8,128)(2,1)} %fusion.163, f32[256,512]{1,0:T(8,128)S(1)} %convolution_add_fusion.3, bf16[256,512]{1,0:T(8,128)(2,1)} %gather_fusion.11, ...), kind=kOutput, calls=%fused_computation.103 | convolution fusion | flops 278921216 | bytes 4196352 | tf_op jit(solution)/shard_map/dot_general | solution.py:50
  97.5 4.0 %collective-permute-done.7 = bf16[1,64,512]{2,1,0:T(8,128)(2,1)S(1)} collective-permute-done((bf16[1,64,512]{2,1,0:T(8,128)(2,1)S(1)}, bf16[1,64,512]{2,1,0:T(8,128)(2,1)S(1)}, u32[]{:S(2)}, u32[]{:S(2)}) %collective-permute-start.7) | collective-permute-done | bytes 65568 | tf_op jit(solution)/shard_map/ppermute | solution.py:19
  104.4 4.8 %collective-permute-done.9 = bf16[128,512]{1,0:T(8,128)(2,1)S(1)} collective-permute-done((bf16[128,512]{1,0:T(8,128)(2,1)S(1)}, bf16[128,512]{1,0:T(8,128)(2,1)S(1)}, u32[]{:S(2)}, u32[]{:S(2)}) %collective-permute-start.9) | collective-permute-done | bytes 131104 | tf_op jit(solution)/shard_map/ppermute | solution.py:158
  110.7 5.5 %collective-permute-done.10 = bf16[256,512]{1,0:T(8,128)(2,1)S(1)} collective-permute-done((bf16[256,512]{1,0:T(8,128)(2,1)S(1)}, bf16[256,512]{1,0:T(8,128)(2,1)S(1)}, u32[]{:S(2)}, u32[]{:S(2)}) %collective-permute-start.10) | collective-permute-done | bytes 262176 | tf_op jit(solution)/shard_map/ppermute | solution.py:158
  120.3 21.2 %collective-permute-done.11 = bf16[512,512]{1,0:T(8,128)(2,1)S(1)} collective-permute-done((bf16[512,512]{1,0:T(8,128)(2,1)S(1)}, bf16[512,512]{1,0:T(8,128)(2,1)S(1)}, u32[]{:S(2)}, u32[]{:S(2)}) %collective-permute-start.11) | collective-permute-done | bytes 524320 | tf_op jit(solution)/shard_map/ppermute | solution.py:158
  148.4 2.9 %collective-permute-start.12 = (bf16[1,64,512]{2,1,0:T(8,128)(2,1)S(1)}, bf16[1,64,512]{2,1,0:T(8,128)(2,1)S(1)}, u32[]{:S(2)}, u32[]{:S(2)}) collective-permute-start(bf16[1,64,512]{2,1,0:T(8,128)(2,1)S(1)} %fusion.70), channel_id=1, source_target_pairs={{0,1},{1,2},{2,3},{3,4},{4,5},{5,6},{6,7},{7,8},{8,9},{9,10},{10,1... | collective-permute-start | bytes 196616 | tf_op jit(solution)/shard_map/ppermute | solution.py:17
  151.4 2.5 %collective-permute-start.13 = (bf16[1,64,512]{2,1,0:T(8,128)(2,1)S(1)}, bf16[1,64,512]{2,1,0:T(8,128)(2,1)S(1)}, u32[]{:S(2)}, u32[]{:S(2)}) collective-permute-start(bf16[1,64,512]{2,1,0:T(8,128)(2,1)S(1)} %fusion.70), channel_id=1, source_target_pairs={{1,0},{2,1},{3,2},{4,3},{5,4},{6,5},{7,6},{8,7},{9,8},{10,9},{11,1... | collective-permute-start | bytes 196616 | tf_op jit(solution)/shard_map/ppermute | solution.py:19
  153.9 3.9 %collective-permute-done.13 = bf16[1,64,512]{2,1,0:T(8,128)(2,1)S(1)} collective-permute-done((bf16[1,64,512]{2,1,0:T(8,128)(2,1)S(1)}, bf16[1,64,512]{2,1,0:T(8,128)(2,1)S(1)}, u32[]{:S(2)}, u32[]{:S(2)}) %collective-permute-start.13) | collective-permute-done | bytes 65568 | tf_op jit(solution)/shard_map/ppermute | solution.py:19
  165.5 4.8 %collective-permute-done.15 = bf16[1,128,512]{2,1,0:T(8,128)(2,1)S(1)} collective-permute-done((bf16[1,128,512]{2,1,0:T(8,128)(2,1)S(1)}, bf16[1,128,512]{2,1,0:T(8,128)(2,1)S(1)}, u32[]{:S(2)}, u32[]{:S(2)}) %collective-permute-start.15) | collective-permute-done | bytes 131104 | tf_op jit(solution)/shard_map/ppermute | solution.py:19
  170.3 4.0 %gather_fusion.19 = bf16[1024,512]{1,0:T(8,128)(2,1)S(1)} fusion(bf16[512,512]{1,0:T(8,128)(2,1)S(1)} %bitcast.208, s32[1024]{0:T(1024)S(1)} %get-tuple-element.51), kind=kCustom, calls=%fused_computation.19 | custom fusion | bytes 2101248 | tf_op jit(solution)/shard_map/gather | solution.py:105
  174.3 4.3 %add_convert_fusion = bf16[1024,512]{1,0:T(8,128)(2,1)} fusion(bf16[1024,512]{1,0:T(8,128)(2,1)} %copy-done.18, bf16[1024,512]{1,0:T(8,128)(2,1)S(1)} %gather_fusion.19, f32[512]{0:T(512)S(1)} %bitcast.239, bf16[2,512,512]{2,1,0:T(8,128)(2,1)S(1)} %copy-done.16, bf16[2,512,512]{2,1,0:T(8,128)(2,1)} %param.40), kind=kOutput, calls=%fused_computation.91 | convolution fusion | flops 1081606144 | bytes 5244928 | tf_op jit(solution)/shard_map/dot_general | solution.py:112
  (136 shorter events, 55.7 us)
Async XLA Ops:
  0.6 96.8 %copy-start = (s32[1024,6]{0,1:T(8,128)S(1)}, s32[1024,6]{0,1:T(8,128)}, u32[]{:S(2)}) copy-start(s32[1024,6]{0,1:T(8,128)} %param.29) | copy-start | bytes 73732
  2.9 9.2 %copy-start.15 = (s32[256]{0:T(256)S(1)}, s32[256]{0:T(256)}, u32[]{:S(2)}) copy-start(s32[256]{0:T(256)} %param.31) | copy-start | bytes 3076
  2.9 9.2 %copy-start.11 = (f32[3,512]{1,0:T(4,128)S(1)}, f32[3,512]{1,0:T(4,128)}, u32[]{:S(2)}) copy-start(f32[3,512]{1,0:T(4,128)} %param.34) | copy-start | bytes 18436
  2.9 9.2 %collective-permute-start = (bf16[1,256,512]{2,1,0:T(8,128)(2,1)S(1)}, bf16[1,256,512]{2,1,0:T(8,128)(2,1)S(1)}, u32[]{:S(2)}, u32[]{:S(2)}) collective-permute-start(bf16[1,256,512]{2,1,0:T(8,128)(2,1)S(1)} %get-tuple-element.57), channel_id=1, source_target_pairs={{0,1},{1,2},{2,3},{3,4},{4,5},{5,6},{6,7},{7,8},{8,9},{9,10},{10,1... | collective-permute-start | bytes 786440 | tf_op jit(solution)/shard_map/ppermute | solution.py:17
  6.8 8.6 %collective-permute-start.1 = (bf16[1,256,512]{2,1,0:T(8,128)(2,1)S(1)}, bf16[1,256,512]{2,1,0:T(8,128)(2,1)S(1)}, u32[]{:S(2)}, u32[]{:S(2)}) collective-permute-start(bf16[1,256,512]{2,1,0:T(8,128)(2,1)S(1)} %get-tuple-element.58), channel_id=1, source_target_pairs={{1,0},{2,1},{3,2},{4,3},{5,4},{6,5},{7,6},{8,7},{9,8},{10,9},{11,1... | collective-permute-start | bytes 786440 | tf_op jit(solution)/shard_map/ppermute | solution.py:19
  58.6 4.6 %collective-permute-start.2 = (bf16[1,128,512]{2,1,0:T(8,128)(2,1)S(1)}, bf16[1,128,512]{2,1,0:T(8,128)(2,1)S(1)}, u32[]{:S(2)}, u32[]{:S(2)}) collective-permute-start(bf16[1,128,512]{2,1,0:T(8,128)(2,1)S(1)} %get-tuple-element.59), channel_id=1, source_target_pairs={{0,1},{1,2},{2,3},{3,4},{4,5},{5,6},{6,7},{7,8},{8,9},{9,10},{10,1... | collective-permute-start | bytes 393224 | tf_op jit(solution)/shard_map/ppermute | solution.py:17
  60.6 7.2 %collective-permute-start.3 = (bf16[1,128,512]{2,1,0:T(8,128)(2,1)S(1)}, bf16[1,128,512]{2,1,0:T(8,128)(2,1)S(1)}, u32[]{:S(2)}, u32[]{:S(2)}) collective-permute-start(bf16[1,128,512]{2,1,0:T(8,128)(2,1)S(1)} %get-tuple-element.60), channel_id=1, source_target_pairs={{1,0},{2,1},{3,2},{4,3},{5,4},{6,5},{7,6},{8,7},{9,8},{10,9},{11,1... | collective-permute-start | bytes 393224 | tf_op jit(solution)/shard_map/ppermute | solution.py:19
  69.9 6.5 %collective-permute-start.4 = (bf16[1,128,512]{2,1,0:T(8,128)(2,1)S(1)}, bf16[1,128,512]{2,1,0:T(8,128)(2,1)S(1)}, u32[]{:S(2)}, u32[]{:S(2)}) collective-permute-start(bf16[1,128,512]{2,1,0:T(8,128)(2,1)S(1)} %get-tuple-element.63), channel_id=1, source_target_pairs={{0,1},{1,2},{2,3},{3,4},{4,5},{5,6},{6,7},{7,8},{8,9},{9,10},{10,1... | collective-permute-start | bytes 393224 | tf_op jit(solution)/shard_map/ppermute | solution.py:17
  71.9 7.2 %collective-permute-start.5 = (bf16[1,128,512]{2,1,0:T(8,128)(2,1)S(1)}, bf16[1,128,512]{2,1,0:T(8,128)(2,1)S(1)}, u32[]{:S(2)}, u32[]{:S(2)}) collective-permute-start(bf16[1,128,512]{2,1,0:T(8,128)(2,1)S(1)} %get-tuple-element.64), channel_id=1, source_target_pairs={{1,0},{2,1},{3,2},{4,3},{5,4},{6,5},{7,6},{8,7},{9,8},{10,9},{11,1... | collective-permute-start | bytes 393224 | tf_op jit(solution)/shard_map/ppermute | solution.py:19
  92.8 17.9 %copy-start.14 = (f32[2,512]{1,0:T(2,128)S(1)}, f32[2,512]{1,0:T(2,128)}, u32[]{:S(2)}) copy-start(f32[2,512]{1,0:T(2,128)} %param.42) | copy-start | bytes 12292
  93.1 4.4 %collective-permute-start.6 = (bf16[1,64,512]{2,1,0:T(8,128)(2,1)S(1)}, bf16[1,64,512]{2,1,0:T(8,128)(2,1)S(1)}, u32[]{:S(2)}, u32[]{:S(2)}) collective-permute-start(bf16[1,64,512]{2,1,0:T(8,128)(2,1)S(1)} %get-tuple-element.65), channel_id=1, source_target_pairs={{0,1},{1,2},{2,3},{3,4},{4,5},{5,6},{6,7},{7,8},{8,9},{9,10},{10,1... | collective-permute-start | bytes 196616 | tf_op jit(solution)/shard_map/ppermute | solution.py:17
  95.0 6.5 %collective-permute-start.7 = (bf16[1,64,512]{2,1,0:T(8,128)(2,1)S(1)}, bf16[1,64,512]{2,1,0:T(8,128)(2,1)S(1)}, u32[]{:S(2)}, u32[]{:S(2)}) collective-permute-start(bf16[1,64,512]{2,1,0:T(8,128)(2,1)S(1)} %get-tuple-element.66), channel_id=1, source_target_pairs={{1,0},{2,1},{3,2},{4,3},{5,4},{6,5},{7,6},{8,7},{9,8},{10,9},{11,1... | collective-permute-start | bytes 196616 | tf_op jit(solution)/shard_map/ppermute | solution.py:19
  103.0 1.3 collective-permute-start.8
  104.3 5.0 %collective-permute-start.9 = (bf16[128,512]{1,0:T(8,128)(2,1)S(1)}, bf16[128,512]{1,0:T(8,128)(2,1)S(1)}, u32[]{:S(2)}, u32[]{:S(2)}) collective-permute-start(bf16[128,512]{1,0:T(8,128)(2,1)S(1)} %maximum_select_fusion.3), channel_id=1, source_target_pairs={{0,2},{1,3},{2,0},{3,1},{4,6},{5,7},{6,4},{7,5},{8,10},{9,11},{10,... | collective-permute-start | bytes 393224 | tf_op jit(solution)/shard_map/ppermute | solution.py:158
  109.3 6.9 %collective-permute-start.10 = (bf16[256,512]{1,0:T(8,128)(2,1)S(1)}, bf16[256,512]{1,0:T(8,128)(2,1)S(1)}, u32[]{:S(2)}, u32[]{:S(2)}) collective-permute-start(bf16[256,512]{1,0:T(8,128)(2,1)S(1)} %maximum_select_fusion.2), channel_id=1, source_target_pairs={{0,4},{1,5},{2,6},{3,7},{4,0},{5,1},{6,2},{7,3},{8,12},{9,13},{10,... | collective-permute-start | bytes 786440 | tf_op jit(solution)/shard_map/ppermute | solution.py:158
  116.5 25.0 %collective-permute-start.11 = (bf16[512,512]{1,0:T(8,128)(2,1)S(1)}, bf16[512,512]{1,0:T(8,128)(2,1)S(1)}, u32[]{:S(2)}, u32[]{:S(2)}) collective-permute-start(bf16[512,512]{1,0:T(8,128)(2,1)S(1)} %maximum_select_fusion.1), channel_id=1, source_target_pairs={{0,8},{1,9},{2,10},{3,11},{4,12},{5,13},{6,14},{7,15},{8,0},{9,1},... | collective-permute-start | bytes 1572872 | tf_op jit(solution)/shard_map/ppermute | solution.py:158
  148.2 12.6 %copy-start.7 = (bf16[64,512]{1,0:T(8,128)(2,1)}, bf16[64,512]{1,0:T(8,128)(2,1)S(1)}, u32[]{:S(2)}) copy-start(bf16[64,512]{1,0:T(8,128)(2,1)S(1)} %fusion.69) | copy-start | bytes 196612
  148.2 10.8 %copy-start.6 = (bf16[256,512]{1,0:T(8,128)(2,1)S(1)}, bf16[256,512]{1,0:T(8,128)(2,1)}, u32[]{:S(2)}) copy-start(bf16[256,512]{1,0:T(8,128)(2,1)} %copy-done.5) | copy-start | bytes 786436
  148.2 10.8 %copy-start.16 = (bf16[2,512,512]{2,1,0:T(8,128)(2,1)S(1)}, bf16[2,512,512]{2,1,0:T(8,128)(2,1)}, u32[]{:S(2)}) copy-start(bf16[2,512,512]{2,1,0:T(8,128)(2,1)} %param.43) | copy-start | bytes 3145732
  148.4 5.5 %collective-permute-start.12 = (bf16[1,64,512]{2,1,0:T(8,128)(2,1)S(1)}, bf16[1,64,512]{2,1,0:T(8,128)(2,1)S(1)}, u32[]{:S(2)}, u32[]{:S(2)}) collective-permute-start(bf16[1,64,512]{2,1,0:T(8,128)(2,1)S(1)} %fusion.70), channel_id=1, source_target_pairs={{0,1},{1,2},{2,3},{3,4},{4,5},{5,6},{6,7},{7,8},{8,9},{9,10},{10,1... | collective-permute-start | bytes 196616 | tf_op jit(solution)/shard_map/ppermute | solution.py:17
  151.4 6.5 %collective-permute-start.13 = (bf16[1,64,512]{2,1,0:T(8,128)(2,1)S(1)}, bf16[1,64,512]{2,1,0:T(8,128)(2,1)S(1)}, u32[]{:S(2)}, u32[]{:S(2)}) collective-permute-start(bf16[1,64,512]{2,1,0:T(8,128)(2,1)S(1)} %fusion.70), channel_id=1, source_target_pairs={{1,0},{2,1},{3,2},{4,3},{5,4},{6,5},{7,6},{8,7},{9,8},{10,9},{11,1... | collective-permute-start | bytes 196616 | tf_op jit(solution)/shard_map/ppermute | solution.py:19
  160.8 13.5 %copy-start.17 = (bf16[256,512]{1,0:T(8,128)(2,1)}, bf16[256,512]{1,0:T(8,128)(2,1)S(1)}, u32[]{:S(2)}) copy-start(bf16[256,512]{1,0:T(8,128)(2,1)S(1)} %fusion.67) | copy-start | bytes 786436
  161.1 4.3 %collective-permute-start.14 = (bf16[1,128,512]{2,1,0:T(8,128)(2,1)S(1)}, bf16[1,128,512]{2,1,0:T(8,128)(2,1)S(1)}, u32[]{:S(2)}, u32[]{:S(2)}) collective-permute-start(bf16[1,128,512]{2,1,0:T(8,128)(2,1)S(1)} %get-tuple-element.61), channel_id=1, source_target_pairs={{0,1},{1,2},{2,3},{3,4},{4,5},{5,6},{6,7},{7,8},{8,9},{9,10},{10,1... | collective-permute-start | bytes 393224 | tf_op jit(solution)/shard_map/ppermute | solution.py:17
  163.0 7.2 %collective-permute-start.15 = (bf16[1,128,512]{2,1,0:T(8,128)(2,1)S(1)}, bf16[1,128,512]{2,1,0:T(8,128)(2,1)S(1)}, u32[]{:S(2)}, u32[]{:S(2)}) collective-permute-start(bf16[1,128,512]{2,1,0:T(8,128)(2,1)S(1)} %get-tuple-element.62), channel_id=1, source_target_pairs={{1,0},{2,1},{3,2},{4,3},{5,4},{6,5},{7,6},{8,7},{9,8},{10,9},{11,1... | collective-permute-start | bytes 393224 | tf_op jit(solution)/shard_map/ppermute | solution.py:19
  (11 other events, 70.4 us)
